TPU v7x, 512 devices: a whole 4x8x8 slice. The times are simulated.
512 devices in a mesh: row: 8 (over z_lo, core), col: 8 (over x, z_hi), tm: 8 (over y).
Axes of the slice: x: 4, y: 8, z: 8 (z_hi: 2, z_lo: 4; z = z_hi * 4 + z_lo), core: 2. Of those that a mesh axis runs over, the one named last changes fastest.
Arguments:
- green_occ: bfloat16 [16, 256, 30720], P('tm', 'row', 'col'), may hold values from -6 to 6
- green_virt: bfloat16 [16, 256, 30720], P('tm', 'row', 'col'), may hold values from -6 to 6
- adjoint_w: bfloat16 [16, 256, 30720], P(None, 'row', ('col', 'tm')), may hold values from -6 to 6
- grad_basis: float32 [3, 256], P(None, 'row'), may hold values from -6 to 6
- owner_map: int32 [30720], replicated, may hold values from 0 to 999
- block_offset: int32 [8], P('row'), may hold values from 0 to 30688
Outputs:
- chi_freq: bfloat16 [16, 256, 30720], P(None, 'row', ('col', 'tm'))
- forces: float32 [3, 1000], replicated
All inputs are finite; a program needn't handle non-finite values.
Results may differ from a plain program's by a relative error of at most 0.0085.
Values may be sent and summed in bfloat16 or wider, within the bound.
No kernel may reach another device: no remote copies, remote signals or barrier semaphores. Data moves between devices by JAX's collectives and lax.ppermute only.
A program may use at most 64 MiB of HBM per device.

v0:
```python
import math
import jax
import jax.numpy as jnp
from jax import lax
from jax.sharding import PartitionSpec as P

NG = 30720
NTAU = 16
NATOM = 1000


def cos_table(count):
    steps = jnp.arange(count).astype(jnp.float32)
    tau = 0.1 * jnp.power(jnp.float32(1.35), steps)
    omega = 0.15 * jnp.power(jnp.float32(1.35), steps)
    return jnp.cos(omega[:, None] * tau[None, :]) / 4.0


def on_device(green_occ, green_virt, adjoint_w, grad_basis, owner_map, block_offset):
    table = cos_table(NTAU)
    scale = 1.0 / math.sqrt(NTAU * NG)
    row_count = green_occ.shape[1]
    product = (green_occ.astype(jnp.float32) * green_virt.astype(jnp.float32)).astype(jnp.bfloat16)
    chi_freq = jnp.einsum(
        "kt,tnc->knc",
        table,
        lax.all_to_all(product, "tm", split_axis=2, concat_axis=0, tiled=True).astype(jnp.float32),
        precision=lax.Precision.HIGHEST,
    ).astype(jnp.bfloat16)
    partial_value = (
        jnp.sum(adjoint_w.astype(jnp.float32) * chi_freq.astype(jnp.float32), axis=(0, 2)) * scale
    )
    owners = lax.dynamic_slice_in_dim(owner_map, block_offset[0], row_count, 0)
    onehot = (owners[:, None] == jnp.arange(NATOM)[None, :]).astype(jnp.float32)
    energy = lax.psum(partial_value, ("col", "tm"))
    local_forces = jnp.dot(
        grad_basis * energy[None, :],
        onehot,
        precision=lax.Precision.HIGHEST,
        preferred_element_type=jnp.float32,
    )
    forces = lax.psum(local_forces, "row")
    return (chi_freq, forces)


def solution(mesh):
    in_specs = (
        P("tm", "row", "col"),
        P("tm", "row", "col"),
        P(None, "row", ("col", "tm")),
        P(None, "row"),
        P(),
        P("row"),
    )
    out_specs = (P(None, "row", ("col", "tm")), P())
    return jax.shard_map(
        on_device, mesh=mesh, in_specs=in_specs, out_specs=out_specs, check_vma=False
    )
```

profile of v0, /device:TPU:1, one launch (start us, length us, event | category | flops | bytes accessed | tf_op | source)
XLA Modules:
  0.0 282.4 jit_solution(8296169190990714850)
XLA Ops:
  0.6 1.3 multiply_convert_fusion
  1.9 1.4 copy.16
  3.3 2.5 reshape.19
  5.9 7.7 %all-to-all-start = ((bf16[8,2,15360]{2,1,0:T(2,128)(2,1)}), bf16[8,2,15360]{2,1,0:T(2,128)(2,1)S(1)}, u32[]{:S(2)}, u32[]{:S(2)}) async-start(bf16[8,2,15360]{2,1,0:T(2,128)(2,1)} %reshape.19), calls=%async_computation | async-start | bytes 983040 | tf_op jit(solution)/shard_map/all_to_all | solution.py:27
  14.2 0.8 dynamic_slice.3
  15.0 12.4 %all-to-all-done = bf16[8,2,15360]{2,1,0:T(2,128)(2,1)S(1)} async-done(((bf16[8,2,15360]{2,1,0:T(2,128)(2,1)}), bf16[8,2,15360]{2,1,0:T(2,128)(2,1)S(1)}, u32[]{:S(2)}, u32[]{:S(2)}) %all-to-all-start) | async-done | bytes 491552 | tf_op jit(solution)/shard_map/all_to_all | solution.py:27
  27.4 1.0 reshape.20
  28.4 0.0 copy-start
  28.4 1.5 copy.17
  29.9 0.0 copy-start.1
  29.9 0.4 all_to_all.16
  30.3 0.0 copy-done
  30.4 1.1 multiply_reduce_fusion
  31.5 1.1 copy.19
  32.5 196.4 %psum.14 = f32[32]{0:T(128)S(1)} all-reduce(f32[32]{0:T(128)S(1)} %broadcast_multiply_fusion), channel_id=1, replica_groups=mesh['row'=8,'col'=8,'tm'=8] {'col','tm'}, use_global_device_ids=true, to_apply=%region_1.0 | all-reduce | flops 32 | bytes 256 | tf_op jit(solution)/shard_map/psum | solution.py:35
  228.9 0.0 copy-done.1
  228.9 0.2 fusion
  229.1 53.3 %psum.15 = f32[3,1000]{1,0:T(4,128)} all-reduce(f32[3,1000]{1,0:T(4,128)S(1)} %fusion), channel_id=1, replica_groups=mesh['row'=8,'col'=8,'tm'=8] {'row'}, use_global_device_ids=true, to_apply=%region_2.0 | all-reduce | flops 3000 | bytes 24000 | tf_op jit(solution)/shard_map/psum | solution.py:42
  (2 shorter events, 0.0 us)
Async XLA Ops:
  5.9 21.5 %all-to-all-start = ((bf16[8,2,15360]{2,1,0:T(2,128)(2,1)}), bf16[8,2,15360]{2,1,0:T(2,128)(2,1)S(1)}, u32[]{:S(2)}, u32[]{:S(2)}) async-start(bf16[8,2,15360]{2,1,0:T(2,128)(2,1)} %reshape.19), calls=%async_computation | async-start | bytes 983040 | tf_op jit(solution)/shard_map/all_to_all | solution.py:27
  28.4 2.0 copy-start
  29.9 199.0 %copy-start.1 = (f32[3,32]{1,0:T(4,128)S(1)}, f32[3,32]{1,0:T(4,128)}, u32[]{:S(2)}) copy-start(f32[3,32]{1,0:T(4,128)} %param.9) | copy-start | bytes 1156
where the time goes:
time: 283 us; the launch traced here: 282 us
  blocking collectives  250 us (88%)
  waiting for transfers between devices  12.4 us (4%)
  local copies, waits for them, and re-layouts  8.71 us (3%)
  starting transfers between devices  7.65 us (3%)
    psum x1, blocking collectives, on_device(): energy = lax.psum(partial_value, ('col', 'tm'))  196 us
    psum x1, blocking collectives, on_device(): forces = lax.psum(local_forces, 'row')  53.3 us
    all_to_all x1, waiting for transfers between devices, on_device(): lax.all_to_all(product, 'tm', split_axis=2, concat_axis=0, tiled=True)  12.4 us
    all_to_all x1, starting transfers between devices, on_device(): lax.all_to_all(product, 'tm', split_axis=2, concat_axis=0, tiled=True)  7.65 us
  transfers between devices with their start and end apart: 1, of which 1 were waited for; matrix products, arithmetic and copies ran while one was open for 0% of the time, Pallas kernels for 0%

commit v1 on v0

--- a/solution.py
+++ b/solution.py
@@ -39,7 +39,7 @@
         precision=lax.Precision.HIGHEST,
         preferred_element_type=jnp.float32,
     )
-    forces = lax.psum(local_forces, "row")
+    forces = jnp.sum(lax.all_gather(local_forces, axis_name="row"), axis=0)
     return (chi_freq, forces)
 
 

time: 283 us -> 275 us (0.972)
  blocking collectives: 250 us -> 242 us
    psum x1 -> x0, blocking collectives: 53.3 us -> none  [on_device(): forces = lax.psum(local_forces, 'row')]
    all_gather x0 -> x1, blocking collectives: none -> 45.3 us  [on_device(): forces = jnp.sum(lax.all_gather(local_forces, axis_name='row'), axis=0)]
where the time goes in v1:
time: 275 us
  blocking collectives  242 us (88%)
  waiting for transfers between devices  12.4 us (5%)
  local copies, waits for them, and re-layouts  8.71 us (3%)
  starting transfers between devices  7.65 us (3%)
    psum x1, blocking collectives, on_device(): energy = lax.psum(partial_value, ('col', 'tm'))  196 us
    all_gather x1, blocking collectives, on_device(): forces = jnp.sum(lax.all_gather(local_forces, axis_name='row'), axis=0)  45.3 us
    all_to_all x1, waiting for transfers between devices, on_device(): lax.all_to_all(product, 'tm', split_axis=2, concat_axis=0, tiled=True)  12.4 us
    all_to_all x1, starting transfers between devices, on_device(): lax.all_to_all(product, 'tm', split_axis=2, concat_axis=0, tiled=True)  7.65 us
  transfers between devices with their start and end apart: 1, of which 1 were waited for; matrix products, arithmetic and copies ran while one was open for 0% of the time, Pallas kernels for 0%

profile of v1, /device:TPU:1, one launch (start us, length us, event | category | flops | bytes accessed | tf_op | source)
XLA Modules:
  0.0 275.1 jit_solution(2470787601660696427)
XLA Ops:
  0.6 1.3 multiply_convert_fusion
  1.9 1.4 copy.16
  3.3 2.5 reshape.23
  5.9 7.7 %all-to-all-start = ((bf16[8,2,15360]{2,1,0:T(2,128)(2,1)}), bf16[8,2,15360]{2,1,0:T(2,128)(2,1)S(1)}, u32[]{:S(2)}, u32[]{:S(2)}) async-start(bf16[8,2,15360]{2,1,0:T(2,128)(2,1)} %reshape.23), calls=%async_computation | async-start | bytes 983040 | tf_op jit(solution)/shard_map/all_to_all | solution.py:27
  14.2 0.8 dynamic_slice.3
  15.0 12.4 %all-to-all-done = bf16[8,2,15360]{2,1,0:T(2,128)(2,1)S(1)} async-done(((bf16[8,2,15360]{2,1,0:T(2,128)(2,1)}), bf16[8,2,15360]{2,1,0:T(2,128)(2,1)S(1)}, u32[]{:S(2)}, u32[]{:S(2)}) %all-to-all-start) | async-done | bytes 491552 | tf_op jit(solution)/shard_map/all_to_all | solution.py:27
  27.4 1.0 reshape.24
  28.4 0.0 copy-start
  28.4 1.5 copy.17
  29.9 0.0 copy-start.1
  29.9 0.4 all_to_all.16
  30.3 0.0 copy-done
  30.4 1.1 multiply_reduce_fusion
  31.5 1.1 copy.19
  32.5 196.4 %psum.7 = f32[32]{0:T(128)S(1)} all-reduce(f32[32]{0:T(128)S(1)} %broadcast_multiply_fusion), channel_id=1, replica_groups=mesh['row'=8,'col'=8,'tm'=8] {'col','tm'}, use_global_device_ids=true, to_apply=%region_1.0 | all-reduce | flops 32 | bytes 256 | tf_op jit(solution)/shard_map/psum | solution.py:35
  228.9 0.0 copy-done.1
  228.9 0.2 convolution_bitcast_fusion
  229.1 45.3 %all-gather.1 = f32[8,3,1000]{2,1,0:T(4,128)S(1)} all-gather(f32[1,3,1000]{2,1,0:T(4,128)S(1)} %convolution_bitcast_fusion), channel_id=2, replica_groups=mesh['row'=8,'col'=8,'tm'=8] {'row'}, dimensions={0}, use_global_device_ids=true | all-gather | bytes 108000 | tf_op jit(solution)/shard_map/all_gather | solution.py:42
  274.5 0.6 reduce_sum.19
  (2 shorter events, 0.0 us)
Async XLA Ops:
  5.9 21.5 %all-to-all-start = ((bf16[8,2,15360]{2,1,0:T(2,128)(2,1)}), bf16[8,2,15360]{2,1,0:T(2,128)(2,1)S(1)}, u32[]{:S(2)}, u32[]{:S(2)}) async-start(bf16[8,2,15360]{2,1,0:T(2,128)(2,1)} %reshape.23), calls=%async_computation | async-start | bytes 983040 | tf_op jit(solution)/shard_map/all_to_all | solution.py:27
  28.4 2.0 copy-start
  29.9 199.0 %copy-start.1 = (f32[3,32]{1,0:T(4,128)S(1)}, f32[3,32]{1,0:T(4,128)}, u32[]{:S(2)}) copy-start(f32[3,32]{1,0:T(4,128)} %param.9) | copy-start | bytes 1156
